TPU v7x, 32 devices: a whole 2x2x4 slice. The times are simulated.
32 devices in a mesh: dp: 4 (over z), seq: 4 (over y, x), expert: 2 (over core).
Axes of the slice: x: 2, y: 2, z: 4, core: 2. Of those that a mesh axis runs over, the one named last changes fastest.
Arguments:
- block_input: float32 [8, 512, 768], P(('dp', 'expert'), 'seq'), may hold values from -12 to 12
- documents: int32 [8, 512], P(('dp', 'expert')), may hold values from 0 to 2, never falling along the last dimension, each value on 1 to 320 neighbouring positions
- route_experts: int32 [8, 512, 2], P(('dp', 'expert'), 'seq'), may hold values from 0 to 7, all different within a row; in each aligned block of 128 rows (0 to 127, 128 to 255, ..., all dimensions but the last counted through in order) at most 48 rows name the same one
- route_gate: float32 [8, 512, 2], P(('dp', 'expert'), 'seq'), may hold values from 0.25 to 1
- first_gain: bfloat16 [768], P(('dp', 'seq', 'expert')), may hold values from 0.25 to 1.75
- entry_weight: bfloat16 [768, 2304], P(None, ('dp', 'seq', 'expert')), may hold values from -0.21875 to 0.21875
- exit_weight: bfloat16 [768, 768], P(None, ('dp', 'seq', 'expert')), may hold values from -0.875 to 0.875
- position_bias: float32 [32, 12], replicated, may hold values from -4 to 260
- second_gain: bfloat16 [768], P(('dp', 'seq', 'expert')), may hold values from 0.25 to 1.75
- expert_up: bfloat16 [8, 768, 3072], P(('dp', 'expert'), None, 'seq'), may hold values from -0.21875 to 0.21875
- expert_down: bfloat16 [8, 3072, 768], P(('dp', 'expert'), 'seq'), may hold values from -0.109375 to 0.109375
- cotangent: float32 [8, 512, 768], P(('dp', 'expert'), 'seq'), may hold values from -6 to 6
Outputs:
- block_output: float32 [8, 512, 768], P(('dp', 'expert'), 'seq')
- back_input: float32 [8, 512, 768], P(('dp', 'expert'), 'seq')
- back_first_gain: float32 [768], P(('dp', 'seq', 'expert'))
- back_entry: float32 [768, 2304], P(None, ('dp', 'seq', 'expert'))
- back_exit: float32 [768, 768], P(None, ('dp', 'seq', 'expert'))
- back_bias: float32 [32, 12], replicated
- back_second_gain: float32 [768], P(('dp', 'seq', 'expert'))
- back_expert_up: float32 [8, 768, 3072], P(('dp', 'expert'), None, 'seq')
- back_expert_down: float32 [8, 3072, 768], P(('dp', 'expert'), 'seq')
Inputs may be any that keep to these rules, and one draw needn't show every extreme that they name: `route_experts`: in each device's aligned block of 128 tokens no expert is named by more than 48 routes, a bound that some block reaches; a token's two experts differ. `documents`: document numbers never fall along a sequence; no document is longer than five eighths of 512 tokens, and one is that long.
All inputs are finite; a program needn't handle non-finite values.
Results may differ from a plain program's by a relative error of at most 0.014.
Values may be sent and summed in bfloat16 or wider, within the bound.
No kernel may reach another device: no remote copies, remote signals or barrier semaphores. Data moves between devices by JAX's collectives and lax.ppermute only.
A program may use at most 128 MiB of HBM per device.

v0:
```python
import jax
import jax.numpy as jnp
from jax import lax
from jax.sharding import PartitionSpec as P

EPSILON = 1e-06
SLOPE = 0.7978845608028654
CUBIC = 0.044715
LIMITS = (19, 21, 24, 27, 31, 35, 40, 46, 52, 59, 67, 77, 87, 99, 113)
MASKED = -1e30
HIGH = lax.Precision.HIGHEST


def gelu_value(values):
    return 0.5 * values * (1.0 + jnp.tanh(SLOPE * (values + CUBIC * values * values * values)))


def gelu_slope(values):
    tangent = jnp.tanh(SLOPE * (values + CUBIC * values * values * values))
    return 0.5 * (1.0 + tangent) + 0.5 * values * (1.0 - tangent * tangent) * SLOPE * (
        1.0 + 3.0 * CUBIC * values * values
    )


def bucket_onehot(lag, count):
    bucket = jnp.minimum(lag, 16)
    for threshold in LIMITS:
        bucket = bucket + (lag >= threshold).astype(jnp.int32)
    return (bucket[..., None] == jnp.arange(count, dtype=jnp.int32)).astype(jnp.float32)


def rms_scale(values):
    return lax.rsqrt(jnp.mean(values * values, axis=-1, keepdims=True) + EPSILON)


def contract_rows(left, right):
    return lax.dot_general(
        left, right, (((0,), (0,)), ((), ())), preferred_element_type=jnp.float32
    )


def contract_cols(left, right):
    return lax.dot_general(
        left, right, (((1,), (1,)), ((), ())), preferred_element_type=jnp.float32
    )


def masked_scores(queries, key_heads, bias_block, allowed, factor):
    scores = (
        jnp.einsum("qhd,khd->hqk", queries, key_heads, preferred_element_type=jnp.float32) * factor
        + bias_block
    )
    return jnp.where(allowed[None], scores, MASKED)


def expert_work(rows, upstream, up_weight, down_weight):
    before = jnp.dot(rows, up_weight, preferred_element_type=jnp.float32)
    active = gelu_value(before).astype(jnp.bfloat16)
    result = jnp.dot(active, down_weight, preferred_element_type=jnp.float32)
    back_active = contract_cols(upstream, down_weight)
    back_before = (back_active * gelu_slope(before)).astype(jnp.bfloat16)
    down_grad = contract_rows(active, upstream)
    up_grad = contract_rows(rows, back_before)
    back_rows = contract_cols(back_before, up_weight)
    return (result, back_rows, up_grad, down_grad)


def local(
    block_input,
    documents,
    route_experts,
    route_gate,
    first_gain,
    entry_weight,
    exit_weight,
    position_bias,
    second_gain,
    expert_up,
    expert_down,
    cotangent,
):
    rows_here = block_input.shape[1]
    features = block_input.shape[2]
    head_count = position_bias.shape[1]
    head_size = features // head_count
    factor = head_size ** (-0.5)
    top_count = route_experts.shape[2]
    inputs = block_input.reshape(rows_here, features)
    upstream = cotangent.reshape(rows_here, features)
    gain_one, entry_full, exit_full, gain_two = (
        lax.all_gather(first_gain, ("dp", "seq", "expert"), axis=0, tiled=True),
        lax.all_gather(entry_weight, ("dp", "seq", "expert"), axis=1, tiled=True),
        lax.all_gather(exit_weight, ("dp", "seq", "expert"), axis=1, tiled=True),
        lax.all_gather(second_gain, ("dp", "seq", "expert"), axis=0, tiled=True),
    )
    gain_one = gain_one.astype(jnp.float32)
    gain_two = gain_two.astype(jnp.float32)
    scale_one = rms_scale(inputs)
    normed_one = (inputs * scale_one * gain_one).astype(jnp.bfloat16)
    projected = jnp.dot(normed_one, entry_full, preferred_element_type=jnp.float32).astype(
        jnp.bfloat16
    )
    queries = projected[:, :features].reshape(rows_here, head_count, head_size)
    key_value = lax.all_gather(projected[:, features:], "seq", axis=0, tiled=True)
    seq_length = key_value.shape[0]
    key_heads = key_value[:, :features].reshape(seq_length, head_count, head_size)
    values = key_value[:, features:].reshape(seq_length, head_count, head_size)
    offset = lax.axis_index("seq") * rows_here
    query_index = offset + jnp.arange(rows_here, dtype=jnp.int32)
    key_index = jnp.arange(seq_length, dtype=jnp.int32)
    segment_keys = documents.reshape(seq_length)
    segment_queries = lax.dynamic_slice_in_dim(segment_keys, offset, rows_here)
    allowed = (key_index[None, :] <= query_index[:, None]) & (
        segment_queries[:, None] == segment_keys[None, :]
    )
    lag_table = jnp.maximum(query_index[:, None] - key_index[None, :], 0)
    bucket_hot = bucket_onehot(lag_table, position_bias.shape[0])
    bias_block = jnp.einsum("qkb,bh->hqk", bucket_hot, position_bias, precision=HIGH)
    scores = masked_scores(queries, key_heads, bias_block, allowed, factor)
    row_peak = jnp.max(scores, axis=2, keepdims=True)
    log_total = row_peak + jnp.log(jnp.sum(jnp.exp(scores - row_peak), axis=2, keepdims=True))
    weights = jnp.where(allowed[None], jnp.exp(scores - log_total), 0.0).astype(jnp.bfloat16)
    context = (
        jnp.einsum("hqk,khd->qhd", weights, values, preferred_element_type=jnp.float32)
        .astype(jnp.bfloat16)
        .reshape(rows_here, features)
    )
    hidden = inputs + jnp.dot(context, exit_full, preferred_element_type=jnp.float32)
    scale_two = rms_scale(hidden)
    normed_two = (hidden * scale_two * gain_two).astype(jnp.bfloat16)
    group_size = lax.axis_size(("dp", "expert"))
    capacity = 3 * rows_here // group_size
    route_count = rows_here * top_count
    flat_routes = route_experts.reshape(route_count)
    flat_gates = route_gate.reshape(route_count)
    member = (flat_routes[:, None] == jnp.arange(group_size, dtype=jnp.int32)[None, :]).astype(
        jnp.int32
    )
    route_rank = jnp.sum(member * (jnp.cumsum(member, axis=0) - 1), axis=1)
    slot_of = flat_routes * capacity + route_rank
    filler = (
        jnp.full((group_size * capacity,), -1, jnp.int32)
        .at[slot_of]
        .set(jnp.arange(route_count, dtype=jnp.int32))
    )
    present = filler >= 0
    source = jnp.maximum(filler, 0)
    token_of = source // top_count
    send_rows = jnp.where(present[:, None], normed_two[token_of], jnp.zeros((), jnp.bfloat16))
    send_upstream = jnp.where(
        present[:, None], upstream[token_of] * flat_gates[source][:, None], 0.0
    ).astype(jnp.bfloat16)
    shaped = (group_size, capacity, features)
    arrived_input, arrived_upstream = (
        lax.all_to_all(
            send_rows.reshape(shaped), ("dp", "expert"), split_axis=0, concat_axis=0, tiled=True
        ),
        lax.all_to_all(
            send_upstream.reshape(shaped), ("dp", "expert"), split_axis=0, concat_axis=0, tiled=True
        ),
    )
    rows_flat = arrived_input.reshape(group_size * capacity, features)
    upstream_flat = arrived_upstream.reshape(group_size * capacity, features)
    full_up, full_down = (
        lax.all_gather(expert_up, "seq", axis=2, tiled=True),
        lax.all_gather(expert_down, "seq", axis=1, tiled=True),
    )
    result, back_rows, up_grad, down_grad = expert_work(
        rows_flat, upstream_flat, full_up[0], full_down[0]
    )
    up_share, down_share = (
        lax.psum_scatter(
            up_grad[None].astype(jnp.bfloat16), "seq", scatter_dimension=2, tiled=True
        ).astype(jnp.float32),
        lax.psum_scatter(
            down_grad[None].astype(jnp.bfloat16), "seq", scatter_dimension=1, tiled=True
        ).astype(jnp.float32),
    )
    returned_out, returned_back = (
        lax.all_to_all(
            result.astype(jnp.bfloat16).reshape(shaped),
            ("dp", "expert"),
            split_axis=0,
            concat_axis=0,
            tiled=True,
        ),
        lax.all_to_all(
            back_rows.astype(jnp.bfloat16).reshape(shaped),
            ("dp", "expert"),
            split_axis=0,
            concat_axis=0,
            tiled=True,
        ),
    )
    route_out = (
        returned_out.reshape(group_size * capacity, features)[slot_of]
        .astype(jnp.float32)
        .reshape(rows_here, top_count, features)
    )
    mixture = jnp.sum(route_out * route_gate.reshape(rows_here, top_count, 1), axis=1)
    block_output = hidden + mixture
    route_back = (
        returned_back.reshape(group_size * capacity, features)[slot_of]
        .astype(jnp.float32)
        .reshape(rows_here, top_count, features)
    )
    back_normed_two = jnp.sum(route_back, axis=1)
    upper_two = back_normed_two * gain_two
    gain_two_grad = jnp.sum(back_normed_two * hidden * scale_two, axis=0)
    back_hidden = upstream + scale_two * (
        upper_two
        - hidden * scale_two * scale_two * jnp.mean(upper_two * hidden, axis=1, keepdims=True)
    )
    entry_back, exit_back = (
        lax.all_gather(entry_weight, ("dp", "seq", "expert"), axis=1, tiled=True),
        lax.all_gather(exit_weight, ("dp", "seq", "expert"), axis=1, tiled=True),
    )
    upstream_hidden = back_hidden.astype(jnp.bfloat16)
    exit_grad = contract_rows(context, upstream_hidden)
    back_context = (
        contract_cols(upstream_hidden, exit_back)
        .astype(jnp.bfloat16)
        .reshape(rows_here, head_count, head_size)
    )
    scores_again = masked_scores(queries, key_heads, bias_block, allowed, factor)
    probs = jnp.where(allowed[None], jnp.exp(scores_again - log_total), 0.0)
    back_probs = jnp.einsum(
        "qhd,khd->hqk", back_context, values, preferred_element_type=jnp.float32
    )
    row_dot = jnp.sum(probs * back_probs, axis=2, keepdims=True)
    back_scores = probs * (back_probs - row_dot)
    bias_grad = jnp.einsum("hqk,qkb->bh", back_scores, bucket_hot, precision=HIGH)
    scaled_back = (back_scores * factor).astype(jnp.bfloat16)
    back_queries = jnp.einsum(
        "hqk,khd->qhd", scaled_back, key_heads, preferred_element_type=jnp.float32
    ).reshape(rows_here, features)
    back_keys = jnp.einsum(
        "hqk,qhd->khd", scaled_back, queries, preferred_element_type=jnp.float32
    ).reshape(seq_length, features)
    back_values = jnp.einsum(
        "hqk,qhd->khd", probs.astype(jnp.bfloat16), back_context, preferred_element_type=jnp.float32
    ).reshape(seq_length, features)
    back_pairs = lax.psum_scatter(
        jnp.concatenate([back_keys, back_values], axis=1).astype(jnp.bfloat16),
        "seq",
        scatter_dimension=0,
        tiled=True,
    ).astype(jnp.float32)
    back_projected = jnp.concatenate([back_queries, back_pairs], axis=1).astype(jnp.bfloat16)
    entry_grad = contract_rows(normed_one, back_projected)
    back_normed_one = contract_cols(back_projected, entry_back)
    upper_one = back_normed_one * gain_one
    gain_one_grad = jnp.sum(back_normed_one * inputs * scale_one, axis=0)
    back_input = back_hidden + scale_one * (
        upper_one
        - inputs * scale_one * scale_one * jnp.mean(upper_one * inputs, axis=1, keepdims=True)
    )
    gain_one_share, entry_share, exit_share, gain_two_share = (
        lax.psum_scatter(gain_one_grad, ("dp", "seq", "expert"), scatter_dimension=0, tiled=True),
        lax.psum_scatter(entry_grad, ("dp", "seq", "expert"), scatter_dimension=1, tiled=True),
        lax.psum_scatter(exit_grad, ("dp", "seq", "expert"), scatter_dimension=1, tiled=True),
        lax.psum_scatter(gain_two_grad, ("dp", "seq", "expert"), scatter_dimension=0, tiled=True),
    )
    bias_total = lax.psum(bias_grad, ("dp", "seq", "expert"))
    return (
        block_output.reshape(block_input.shape),
        back_input.reshape(block_input.shape),
        gain_one_share,
        entry_share,
        exit_share,
        bias_total,
        gain_two_share,
        up_share,
        down_share,
    )


def solution(mesh):
    placed = (
        P(("dp", "expert"), "seq", None),
        P(("dp", "expert"), None),
        P(("dp", "expert"), "seq", None),
        P(("dp", "expert"), "seq", None),
        P(("dp", "seq", "expert")),
        P(None, ("dp", "seq", "expert")),
        P(None, ("dp", "seq", "expert")),
        P(),
        P(("dp", "seq", "expert")),
        P(("dp", "expert"), None, "seq"),
        P(("dp", "expert"), "seq", None),
        P(("dp", "expert"), "seq", None),
    )
    return jax.shard_map(
        local,
        mesh=mesh,
        in_specs=placed,
        out_specs=(
            P(("dp", "expert"), "seq", None),
            P(("dp", "expert"), "seq", None),
            P(("dp", "seq", "expert")),
            P(None, ("dp", "seq", "expert")),
            P(None, ("dp", "seq", "expert")),
            P(),
            P(("dp", "seq", "expert")),
            P(("dp", "expert"), None, "seq"),
            P(("dp", "expert"), "seq", None),
        ),
        check_vma=False,
    )
```

profile of v0, /device:TPU:0, one launch (start us, length us, event | category | flops | bytes accessed | tf_op | source)
XLA Modules:
  0.0 738.7 jit_solution(6812603287576350508)
XLA Ops:
  9.7 42.8 %all-reduce.5 = (bf16[768]{0:T(1024)(128)(2,1)S(1)}, bf16[768]{0:T(1024)(128)(2,1)S(1)}) all-reduce(bf16[768]{0:T(1024)(128)(2,1)S(1)} %dynamic-update-slice, bf16[768]{0:T(1024)(128)(2,1)S(1)} %dynamic-update-slice.1), channel_id=1, replica_groups=mesh['dp'=4,'seq'=4,'expert'=2] {'dp','seq','expert'}, use_global_device_ids=true, to_apply=%add | all-reduce | flops 1536 | bytes 6144
  53.6 20.0 %all-gather.6.cloned.1.call-done = bf16[768,2304]{0,1:T(8,128)(2,1)} async-done(((bf16[768,72]{0,1:T(8,128)(2,1)}), bf16[768,2304]{0,1:T(8,128)(2,1)}) %all-gather.6.cloned.1.call-update) | async-done | bytes 3538960 | tf_op jit(solution)/shard_map/all_gather | solution.py:92
  73.6 3.4 convolution_convert_fusion.2
  82.3 4.1 fusion.1
  86.4 3.5 copy.51
  95.3 13.1 %all-gather.8.cloned.1.call-done = bf16[512,1536]{1,0:T(8,128)(2,1)} async-done(((bf16[128,1536]{1,0:T(8,128)(2,1)}), bf16[512,1536]{1,0:T(8,128)(2,1)}) %all-gather.8.cloned.1.call-update) | async-done | bytes 1572880 | tf_op jit(solution)/shard_map/all_gather | solution.py:104
  108.4 2.6 fusion.72
  111.0 2.3 copy.49
  113.3 2.3 copy.47
  115.6 2.0 fusion.73
  120.2 45.1 %all-gather.10.cloned.1.call-done = bf16[768,768]{0,1:T(8,128)(2,1)} async-done(((bf16[768,24]{0,1:T(8,128)(2,1)}), bf16[768,768]{0,1:T(8,128)(2,1)}) %all-gather.10.cloned.1.call-update) | async-done | bytes 1179664 | tf_op jit(solution)/shard_map/all_gather | solution.py:93
  165.3 1.9 multiply_reduce_fusion.4
  167.4 2.2 gather_fusion
  170.5 4.0 all-to-all-start
  174.6 1.9 gather_fusion.2
  176.8 2.8 gather_fusion.3
  180.6 10.6 %all-to-all-done = bf16[8,48,768]{2,1,0:T(8,128)(2,1)S(1)} async-done(((bf16[8,48,768]{2,1,0:T(8,128)(2,1)}), bf16[8,48,768]{2,1,0:T(8,128)(2,1)S(1)}, u32[]{:S(2)}, u32[]{:S(2)}) %all-to-all-start) | async-done | bytes 589856 | tf_op jit(solution)/shard_map/all_to_all | solution.py:155
  191.2 3.5 all-to-all-start.2
  194.8 28.1 %all-gather.12.cloned.1.call-done = bf16[1,768,3072]{2,1,0:T(8,128)(2,1)} async-done(((bf16[1,768,768]{2,1,0:T(8,128)(2,1)}), bf16[1,768,3072]{2,1,0:T(8,128)(2,1)}) %all-gather.12.cloned.1.call-update) | async-done | bytes 4718608 | tf_op jit(solution)/shard_map/all_gather | solution.py:165
  222.9 6.5 fusion.15
  229.4 52.1 %all-gather.14.cloned.1.call-done = bf16[1,3072,768]{2,1,0:T(8,128)(2,1)} async-done(((bf16[1,768,768]{2,1,0:T(8,128)(2,1)}), bf16[1,3072,768]{2,1,0:T(8,128)(2,1)}) %all-gather.14.cloned.1.call-update) | async-done | bytes 4718608 | tf_op jit(solution)/shard_map/all_gather | solution.py:166
  281.5 7.7 %fusion.8 = bf16[384,3072]{1,0:T(8,128)(2,1)S(1)} fusion(f32[384,3072]{1,0:T(8,128)} %fusion.15, bf16[384,768]{1,0:T(8,128)(2,1)S(1)} %bitcast.134, bf16[1,3072,768]{2,1,0:T(8,128)(2,1)} %all-gather.14.cloned.1.call-done), kind=kOutput, calls=%fused_computation.19 | convolution fusion | flops 1834352640 | bytes 12386304 | tf_op jit(solution)/shard_map/dot_general | solution.py:43
  289.2 2.9 fusion.25
  292.1 4.6 all-to-all-start.3
  296.7 7.4 %fusion.28 = bf16[384,768]{1,0:T(8,128)(2,1)} fusion(bf16[1,3072,768]{2,1,0:T(8,128)(2,1)} %all-gather.14.cloned.1.call-done, f32[384,3072]{1,0:T(8,128)} %fusion.15), kind=kOutput, calls=%fused_computation.46 | convolution fusion | flops 1822851072 | bytes 10027008 | tf_op jit(solution)/shard_map/dot_general | solution.py:59
  304.1 9.3 %all-to-all-done.3 = bf16[8,48,768]{2,1,0:T(8,128)(2,1)S(1)} async-done(((bf16[8,48,768]{2,1,0:T(8,128)(2,1)}), bf16[8,48,768]{2,1,0:T(8,128)(2,1)S(1)}, u32[]{:S(2)}, u32[]{:S(2)}) %all-to-all-start.3) | async-done | bytes 589856 | tf_op jit(solution)/shard_map/all_to_all | solution.py:187
  313.4 3.5 all-to-all-start.1
  321.7 11.9 %all-to-all-done.1 = bf16[8,48,768]{2,1,0:T(8,128)(2,1)S(1)} async-done(((bf16[8,48,768]{2,1,0:T(8,128)(2,1)}), bf16[8,48,768]{2,1,0:T(8,128)(2,1)S(1)}, u32[]{:S(2)}, u32[]{:S(2)}) %all-to-all-start.1) | async-done | bytes 589856 | tf_op jit(solution)/shard_map/all_to_all | solution.py:180
  336.1 2.3 multiply_reduce_fusion.1
  338.4 2.1 multiply_add_fusion.1
  341.2 1.6 convolution_convert_fusion.6
  343.0 2.4 multiply_reduce_fusion
  347.1 1.7 copy-done.5
  350.9 6.0 fusion.17
  358.0 7.6 %fusion.18 = bf16[1,3072,768]{2,1,0:T(8,128)(2,1)} fusion(bf16[384,768]{1,0:T(8,128)(2,1)S(1)} %bitcast.135, f32[384,3072]{1,0:T(8,128)} %fusion.15), kind=kOutput, calls=%fused_computation.30 | convolution fusion | flops 1824915456 | bytes 10027008 | tf_op jit(solution)/shard_map/dot_general | solution.py:37
  366.6 3.0 fusion.57
  369.7 2.5 convolution_convert_fusion.5
  372.2 7.9 %reduce-scatter.16.cloned.1.call-done = bf16[128,1536]{1,0:T(8,128)(2,1)} async-done(((bf16[512,1536]{1,0:T(8,128)(2,1)}), bf16[128,1536]{1,0:T(8,128)(2,1)}) %reduce-scatter.16.cloned.1.call-update) | async-done | bytes 393232
  380.1 1.9 copy.60
  382.0 5.1 fusion.36
  387.2 3.6 copy.58
  390.8 6.3 fusion.31
  397.9 41.0 %all-reduce.4 = (f32[768]{0:T(1024)S(1)}, f32[32,12]{0,1:T(8,128)}, f32[768]{0:T(1024)S(1)}) all-reduce(f32[768]{0:T(1024)S(1)} %get-tuple-element.11, f32[32,12]{0,1:T(8,128)S(1)} %fusion.31, f32[768]{0:T(1024)S(1)} %copy-done.33), channel_id=3, replica_groups=mesh['dp'=4,'seq'=4,'expert'=2] {'dp','seq','expert'}, use_global_device_ids=true, to_apply=%region_15.16.clone | all-reduce | flops 1920 | bytes 15360
  441.4 2.8 convert_element_type.234
  444.3 57.2 %reduce-scatter.14.cloned.1.call-done = bf16[1,768,768]{2,1,0:T(8,128)(2,1)} async-done(((bf16[1,3072,768]{2,1,0:T(8,128)(2,1)}), bf16[1,768,768]{2,1,0:T(8,128)(2,1)}) %reduce-scatter.14.cloned.1.call-update) | async-done | bytes 1179664 | tf_op jit(solution)/shard_map/reduce_scatter | solution.py:175
  501.5 2.8 convert_element_type.237
  504.3 102.7 %reduce-scatter.10.cloned.1.call-done = f32[768,24]{0,1:T(8,128)} async-done(((f32[768,768]{0,1:T(8,128)}), f32[768,24]{0,1:T(8,128)}) %reduce-scatter.10.cloned.1.call-update) | async-done | bytes 73744 | tf_op jit(solution)/shard_map/reduce_scatter | solution.py:261
  607.0 124.6 %reduce-scatter.8.cloned.1.call-done = f32[768,72]{0,1:T(8,128)} async-done(((f32[768,2304]{0,1:T(8,128)}), f32[768,72]{0,1:T(8,128)}) %reduce-scatter.8.cloned.1.call-update) | async-done | bytes 221200 | tf_op jit(solution)/shard_map/reduce_scatter | solution.py:260
  (179 shorter events, 36.4 us)
Async XLA Ops:
  7.2 75.1 %copy-start = (f32[32,12]{0,1:T(8,128)S(1)}, f32[32,12]{0,1:T(8,128)}, u32[]{:S(2)}) copy-start(f32[32,12]{0,1:T(8,128)} %param.19) | copy-start | bytes 4612
  7.2 66.4 %all-gather.6.cloned.1.call-start = ((), (), s32[]{:S(2)}) async-start(), calls=%async_computation.9 | async-start | bytes 3649536 | tf_op jit(solution)/shard_map/all_gather | solution.py:92
  7.9 100.5 %all-gather.8.cloned.1.call-start = ((), (), s32[]{:S(2)}) async-start(), calls=%async_computation.10 | async-start | bytes 1966080 | tf_op jit(solution)/shard_map/all_gather | solution.py:104
  52.5 27.5 %copy-start.29 = (f32[768]{0:T(1024)}, f32[768]{0:T(1024)S(1)}, u32[]{:S(2)}) copy-start(f32[768]{0:T(1024)S(1)} %convert_element_type.196) | copy-start | bytes 9220
  53.6 26.4 %copy-start.35 = (f32[128]{0:T(128)}, f32[128]{0:T(128)S(1)}, u32[]{:S(2)}) copy-start(f32[128]{0:T(128)S(1)} %add_rsqrt_fusion.1) | copy-start | bytes 1540
  53.6 26.9 %copy-start.39 = (s32[1,128,2]{1,2,0:T(2,128)S(1)}, s32[1,128,2]{1,2,0:T(2,128)}, u32[]{:S(2)}) copy-start(s32[1,128,2]{1,2,0:T(2,128)} %param.14) | copy-start | bytes 3076
  78.7 86.6 %all-gather.10.cloned.1.call-start = ((), (), s32[]{:S(2)}) async-start(), calls=%async_computation.11 | async-start | bytes 1216512 | tf_op jit(solution)/shard_map/all_gather | solution.py:93
  79.4 143.5 %all-gather.12.cloned.1.call-start = ((), (), s32[]{:S(2)}) async-start(), calls=%async_computation.12 | async-start | bytes 5898240 | tf_op jit(solution)/shard_map/all_gather | solution.py:165
  80.0 201.5 %all-gather.14.cloned.1.call-start = ((), (), s32[]{:S(2)}) async-start(), calls=%async_computation.13 | async-start | bytes 5898240 | tf_op jit(solution)/shard_map/all_gather | solution.py:166
  86.4 7.4 copy-start.43
  86.4 8.7 %slice-start = ((bf16[128,2304]{1,0:T(8,128)(2,1)}), bf16[128,768]{1,0:T(8,128)(2,1)S(1)}, s32[]{:S(2)}) async-start(bf16[128,2304]{1,0:T(8,128)(2,1)} %copy-done.18), calls=%async_computation.19 | async-start | bytes 393216 | tf_op jit(solution)/shard_map/slice | solution.py:103
  95.3 20.3 %copy-start.20 = (bf16[128,768]{0,1:T(8,128)(2,1)}, bf16[128,768]{0,1:T(8,128)(2,1)S(1)}, u32[]{:S(2)}) copy-start(bf16[128,768]{0,1:T(8,128)(2,1)S(1)} %copy.48) | copy-start | bytes 589828
  95.3 20.3 %copy-start.22 = (pred[128,512]{1,0:T(8,128)(4,1)S(1)}, pred[128,512]{1,0:T(8,128)(4,1)}, u32[]{:S(2)}) copy-start(pred[128,512]{1,0:T(8,128)(4,1)} %fusion.54) | copy-start | bytes 196612
  117.7 47.6 %copy-start.7 = (f32[1,128,768]{2,1,0:T(8,128)S(1)}, f32[1,128,768]{2,1,0:T(8,128)}, u32[]{:S(2)}) copy-start(f32[1,128,768]{2,1,0:T(8,128)} %param.12) | copy-start | bytes 1179652
  119.4 47.9 %copy-start.31 = (f32[768]{0:T(1024)S(1)}, f32[768]{0:T(1024)}, u32[]{:S(2)}) copy-start(f32[768]{0:T(1024)} %convert_element_type.218) | copy-start | bytes 9220
  119.4 48.0 %copy-start.32 = (s32[1024]{0:T(1024)S(1)}, s32[1024]{0:T(1024)}, u32[]{:S(2)}) copy-start(s32[1024]{0:T(1024)} %get-tuple-element.32) | copy-start | bytes 12292
  120.2 47.1 %copy-start.24 = (bf16[12,64,128]{2,1,0:T(8,128)(2,1)}, bf16[12,64,128]{2,1,0:T(8,128)(2,1)S(1)}, u32[]{:S(2)}) copy-start(bf16[12,64,128]{2,1,0:T(8,128)(2,1)S(1)} %convolution_convert_fusion.7) | copy-start | bytes 589828
  167.2 153.2 %copy-start.10 = (f32[128,768]{1,0:T(8,128)}, f32[128,768]{1,0:T(8,128)S(1)}, u32[]{:S(2)}) copy-start(f32[128,768]{1,0:T(8,128)S(1)} %get-tuple-element.27) | copy-start | bytes 1179652
  167.2 2.4 copy-start.42
  167.3 153.2 %copy-start.37 = (f32[128]{0:T(128)}, f32[128]{0:T(128)S(1)}, u32[]{:S(2)}) copy-start(f32[128]{0:T(128)S(1)} %add_rsqrt_fusion) | copy-start | bytes 1540
  167.4 7.2 copy-start.2
  170.5 20.7 %all-to-all-start = ((bf16[8,48,768]{2,1,0:T(8,128)(2,1)}), bf16[8,48,768]{2,1,0:T(8,128)(2,1)S(1)}, u32[]{:S(2)}, u32[]{:S(2)}) async-start(bf16[8,48,768]{2,1,0:T(8,128)(2,1)} %broadcast_select_fusion), calls=%async_computation | async-start | bytes 1179648 | tf_op jit(solution)/shard_map/all_to_all | solution.py:155
  191.2 38.2 %copy-start.25 = (bf16[8,48,768]{2,1,0:T(8,128)(2,1)}, bf16[8,48,768]{2,1,0:T(8,128)(2,1)S(1)}, u32[]{:S(2)}) copy-start(bf16[8,48,768]{2,1,0:T(8,128)(2,1)S(1)} %all-to-all-done) | copy-start | bytes 1769476
  191.2 38.2 %all-to-all-start.2 = ((bf16[8,48,768]{2,1,0:T(8,128)(2,1)}), bf16[8,48,768]{2,1,0:T(8,128)(2,1)S(1)}, u32[]{:S(2)}, u32[]{:S(2)}) async-start(bf16[8,48,768]{2,1,0:T(8,128)(2,1)} %select_convert_fusion), calls=%async_computation.2 | async-start | bytes 1179648 | tf_op jit(solution)/shard_map/all_to_all | solution.py:158
  229.4 59.8 %copy-start.27 = (bf16[8,48,768]{2,1,0:T(8,128)(2,1)}, bf16[8,48,768]{2,1,0:T(8,128)(2,1)S(1)}, u32[]{:S(2)}) copy-start(bf16[8,48,768]{2,1,0:T(8,128)(2,1)S(1)} %all-to-all-done.2) | copy-start | bytes 1769476
  281.5 7.7 %copy-start.44 = (bf16[1,768,3072]{2,1,0:T(8,128)(2,1)S(1)}, bf16[1,768,3072]{2,1,0:T(8,128)(2,1)}, u32[]{:S(2)}) copy-start(bf16[1,768,3072]{2,1,0:T(8,128)(2,1)} %all-gather.12.cloned.1.call-done) | copy-start | bytes 14155780
  289.2 2.9 copy-start.45
  292.1 21.3 %all-to-all-start.3 = ((bf16[8,48,768]{2,1,0:T(8,128)(2,1)}), bf16[8,48,768]{2,1,0:T(8,128)(2,1)S(1)}, u32[]{:S(2)}, u32[]{:S(2)}) async-start(bf16[8,48,768]{2,1,0:T(8,128)(2,1)} %bitcast.25), calls=%async_computation.3 | async-start | bytes 1179648 | tf_op jit(solution)/shard_map/all_to_all | solution.py:187
  296.7 21.2 %copy-start.41 = (s32[256,1]{0,1:T(1,128)S(1)}, s32[256,1]{0,1:T(1,128)}, u32[]{:S(2)}) copy-start(s32[256,1]{0,1:T(1,128)} %copy-done.40) | copy-start | bytes 3076
  313.4 20.2 %all-to-all-start.1 = ((bf16[8,48,768]{2,1,0:T(8,128)(2,1)}), bf16[8,48,768]{2,1,0:T(8,128)(2,1)S(1)}, u32[]{:S(2)}, u32[]{:S(2)}) async-start(bf16[8,48,768]{2,1,0:T(8,128)(2,1)} %bitcast.18), calls=%async_computation.1 | async-start | bytes 1179648 | tf_op jit(solution)/shard_map/all_to_all | solution.py:180
  317.0 63.2 %reduce-scatter.16.cloned.1.call-start = ((), (), s32[]{:S(2)}) async-start(), calls=%async_computation.18 | async-start | bytes 1966080
  320.5 14.4 %copy-start.15 = (f32[128,768]{1,0:T(8,128)}, f32[128,768]{1,0:T(8,128)S(1)}, u32[]{:S(2)}) copy-start(f32[128,768]{1,0:T(8,128)S(1)} %reduce_sum.107) | copy-start | bytes 1179652
  336.1 6.9 copy-start.4
  343.0 2.4 copy-start.23
  346.2 2.6 copy-start.21
  350.9 90.6 %reduce-scatter.12.cloned.1.call-start = ((), (), s32[]{:S(2)}) async-start(), calls=%async_computation.16 | async-start | bytes 5898240 | tf_op jit(solution)/shard_map/reduce_scatter | solution.py:172
  357.0 144.5 %reduce-scatter.14.cloned.1.call-start = ((), (), s32[]{:S(2)}) async-start(), calls=%async_computation.17 | async-start | bytes 5898240 | tf_op jit(solution)/shard_map/reduce_scatter | solution.py:175
  365.6 4.0 copy-start.6
  365.6 241.4 %reduce-scatter.10.cloned.1.call-start = ((), (), s32[]{:S(2)}) async-start(), calls=%async_computation.15 | async-start | bytes 2433024 | tf_op jit(solution)/shard_map/reduce_scatter | solution.py:261
  369.6 12.5 %copy-start.8 = (f32[1,128,768]{2,1,0:T(8,128)S(1)}, f32[1,128,768]{2,1,0:T(8,128)}, u32[]{:S(2)}) copy-start(f32[1,128,768]{2,1,0:T(8,128)} %param.12) | copy-start | bytes 1179652
  369.6 12.5 %copy-start.30 = (f32[768]{0:T(1024)S(1)}, f32[768]{0:T(1024)}, u32[]{:S(2)}) copy-start(f32[768]{0:T(1024)} %copy-done.29) | copy-start | bytes 9220
  369.6 12.5 %copy-start.36 = (f32[128]{0:T(128)S(1)}, f32[128]{0:T(128)}, u32[]{:S(2)}) copy-start(f32[128]{0:T(128)} %copy-done.35) | copy-start | bytes 1540
  369.6 362.1 %reduce-scatter.8.cloned.1.call-start = ((), (), s32[]{:S(2)}) async-start(), calls=%async_computation.14 | async-start | bytes 7299072 | tf_op jit(solution)/shard_map/reduce_scatter | solution.py:260
  390.8 6.3 copy-start.9
  390.8 6.3 copy-start.14
  390.8 6.3 copy-start.19
  397.1 43.0 %copy-start.13 = (f32[128,768]{1,0:T(8,128)S(1)}, f32[128,768]{1,0:T(8,128)}, u32[]{:S(2)}) copy-start(f32[128,768]{1,0:T(8,128)} %copy-done.11) | copy-start | bytes 1179652
  440.1 291.6 %copy-start.1 = (f32[32,12]{0,1:T(8,128)S(1)}, f32[32,12]{0,1:T(8,128)}, u32[]{:S(2)}) copy-start(f32[32,12]{0,1:T(8,128)} %param.19) | copy-start | bytes 4612
  (13 other events, 18.0 us)
Sparse Core Ops, SparseCore 0:
  10.9 62.6 all-gather.5
  78.8 29.6 all-gather.7
  111.3 53.9 all-gather.9
  167.0 55.8 all-gather.11
  224.5 56.9 all-gather.13
  351.0 29.0 reduce-scatter.15
  383.1 58.2 reduce-scatter.11
  444.4 56.9 reduce-scatter.13
  507.3 99.6 reduce-scatter.9
  613.1 118.4 reduce-scatter.7
where the time goes:
time: 748 us; the launch traced here: 739 us
  waiting for transfers between devices  486 us (65%)
  blocking collectives  83.8 us (11%)
  matrix products  73.1 us (10%)
  local copies, waits for them, and re-layouts  43.2 us (6%)
  other arithmetic  21.4 us (3%)
  starting transfers between devices  16.5 us (2%)
  between operations  15.1 us (2%)
    reduce_scatter x1, waiting for transfers between devices, local(): lax.psum_scatter(entry_grad, ('dp', 'seq', 'expert'), scatter_dimension=1...  125 us
    reduce_scatter x1, waiting for transfers between devices, local(): lax.psum_scatter(exit_grad, ('dp', 'seq', 'expert'), scatter_dimension=1,...  103 us
    unnamed x2, blocking collectives  83.8 us
    reduce_scatter x1, waiting for transfers between devices, local(): lax.psum_scatter(down_grad[None].astype(jnp.bfloat16), 'seq', scatter_dim...  57.2 us
    all_gather x1, waiting for transfers between devices, local(): lax.all_gather(expert_down, 'seq', axis=1, tiled=True)  52.1 us
    all_gather x1, waiting for transfers between devices, local(): lax.all_gather(exit_weight, ('dp', 'seq', 'expert'), axis=1, tiled=True)  45.1 us
    all_gather x1, waiting for transfers between devices, local(): lax.all_gather(expert_up, 'seq', axis=2, tiled=True)  28.1 us
    dot_general x4, matrix products, contract_rows(): lax.dot_general(left, right, (((0,), (0,)), ((), ())), preferred_element_...  21.7 us
  transfers between devices with their start and end apart: 14, of which 13 were waited for; matrix products, arithmetic and copies ran while one was open for 14% of the time, Pallas kernels for 0%

commit v1 on v0

--- a/solution.py
+++ b/solution.py
@@ -9,6 +9,28 @@
 LIMITS = (19, 21, 24, 27, 31, 35, 40, 46, 52, 59, 67, 77, 87, 99, 113)
 MASKED = -1e30
 HIGH = lax.Precision.HIGHEST
+
+
+def laid_out(blocks, dim):
+    blocks = jnp.moveaxis(blocks, 0, dim)
+    lengths = blocks.shape
+    return blocks.reshape(*lengths[:dim], lengths[dim] * lengths[dim + 1], *lengths[dim + 2 :])
+
+
+def collect(array, axis, dim):
+    size = lax.axis_size(axis)
+    pairs = [(i, (i + 1) % size) for i in range(size)]
+    back = [(b, a) for a, b in pairs]
+    lower, upper = ([], [])
+    for step in range(size - 1):
+        if step % 2 == 0:
+            lower.append(lax.ppermute(lower[-1] if lower else array, axis, pairs))
+        else:
+            upper.append(lax.ppermute(upper[-1] if upper else array, axis, back))
+    pieces = jnp.stack([*lower[::-1], array, *upper])
+    shift = lax.axis_index(axis) - len(lower)
+    pieces = pieces[(jnp.arange(size) - shift) % size]
+    return laid_out(pieces, dim)
 
 
 def gelu_value(values):
@@ -163,7 +185,7 @@
     upstream_flat = arrived_upstream.reshape(group_size * capacity, features)
     full_up, full_down = (
         lax.all_gather(expert_up, "seq", axis=2, tiled=True),
-        lax.all_gather(expert_down, "seq", axis=1, tiled=True),
+        collect(expert_down, "seq", 1),
     )
     result, back_rows, up_grad, down_grad = expert_work(
         rows_flat, upstream_flat, full_up[0], full_down[0]

time: 748 us -> 723 us (0.967)
  waiting for transfers between devices: 486 us -> 427 us
  local copies, waits for them, and re-layouts: 43.2 us -> 63.8 us
  other arithmetic: 21.4 us -> 31.5 us
    reduce_scatter x1, waiting for transfers between devices: 0.44 us -> 57.2 us  [local(): lax.psum_scatter(up_grad[None].astype(jnp.bfloat16), 'seq', scatter_dimen...]
    reduce_scatter x1, waiting for transfers between devices: 57.2 us -> 0.45 us  [local(): lax.psum_scatter(down_grad[None].astype(jnp.bfloat16), 'seq', scatter_dim...]
    all_gather x1 -> x0, waiting for transfers between devices: 52.1 us -> none  [local(): lax.all_gather(expert_down, 'seq', axis=1, tiled=True)]
    ppermute x0 -> x3, waiting for transfers between devices: none -> 24.9 us  [the longest x2 24.9 us: collect(): lower.append(lax.ppermute(lower[-1] if lower else array, axis, pairs))]
    all_gather x1, waiting for transfers between devices: 13.1 us -> 0.02 us  [local(): lax.all_gather(projected[:, features:], 'seq', axis=0, tiled=True)]
    all_gather x1, waiting for transfers between devices: 28.1 us -> 17 us  [local(): lax.all_gather(expert_up, 'seq', axis=2, tiled=True)]
    all_to_all x1, waiting for transfers between devices: 10.6 us -> 0.01 us  [local(): lax.all_to_all(send_rows.reshape(shaped), ('dp', 'expert'), split_axis=0,...]
    all_gather x1, waiting for transfers between devices: 45.1 us -> 55.1 us  [local(): lax.all_gather(exit_weight, ('dp', 'seq', 'expert'), axis=1, tiled=True)]
  transfers between devices with their start and end apart: 14 -> 16, of which waited for: 13 -> 11; matrix products, arithmetic and copies ran while one was open for 14% -> 18% of each run, Pallas kernels for 0% -> 0%
where the time goes in v1:
time: 723 us; the launch traced here: 713 us
  waiting for transfers between devices  427 us (59%)
  blocking collectives  83.8 us (12%)
  matrix products  69.5 us (10%)
  local copies, waits for them, and re-layouts  63.8 us (9%)
  other arithmetic  31.5 us (4%)
  starting transfers between devices  22.8 us (3%)
  between operations  14.7 us (2%)
    reduce_scatter x1, waiting for transfers between devices, local(): lax.psum_scatter(entry_grad, ('dp', 'seq', 'expert'), scatter_dimension=1...  125 us
    reduce_scatter x1, waiting for transfers between devices, local(): lax.psum_scatter(exit_grad, ('dp', 'seq', 'expert'), scatter_dimension=1,...  103 us
    unnamed x2, blocking collectives  83.8 us
    reduce_scatter x1, waiting for transfers between devices, local(): lax.psum_scatter(up_grad[None].astype(jnp.bfloat16), 'seq', scatter_dimen...  57.2 us
    all_gather x1, waiting for transfers between devices, local(): lax.all_gather(exit_weight, ('dp', 'seq', 'expert'), axis=1, tiled=True)  55.1 us
    ppermute x2, waiting for transfers between devices, collect(): lower.append(lax.ppermute(lower[-1] if lower else array, axis, pairs))  24.9 us
    dot_general x4, matrix products, contract_rows(): lax.dot_general(left, right, (((0,), (0,)), ((), ())), preferred_element_...  21.4 us
    all_gather x1, waiting for transfers between devices, local(): lax.all_gather(entry_weight, ('dp', 'seq', 'expert'), axis=1, tiled=True)  20 us
  transfers between devices with their start and end apart: 16, of which 11 were waited for; matrix products, arithmetic and copies ran while one was open for 18% of the time, Pallas kernels for 0%

profile of v1, /device:TPU:0, one launch (start us, length us, event | category | flops | bytes accessed | tf_op | source)
XLA Modules:
  0.0 713.2 jit_solution(8396130288251240284)
XLA Ops:
  9.7 42.8 %all-reduce.5 = (bf16[768]{0:T(1024)(128)(2,1)S(1)}, bf16[768]{0:T(1024)(128)(2,1)S(1)}) all-reduce(bf16[768]{0:T(1024)(128)(2,1)S(1)} %dynamic-update-slice, bf16[768]{0:T(1024)(128)(2,1)S(1)} %dynamic-update-slice.1), channel_id=1, replica_groups=mesh['dp'=4,'seq'=4,'expert'=2] {'dp','seq','expert'}, use_global_device_ids=true, to_apply=%add | all-reduce | flops 1536 | bytes 6144
  53.6 20.0 %all-gather.5.cloned.1.call-done = bf16[768,2304]{0,1:T(8,128)(2,1)} async-done(((bf16[768,72]{0,1:T(8,128)(2,1)}), bf16[768,2304]{0,1:T(8,128)(2,1)}) %all-gather.5.cloned.1.call-update) | async-done | bytes 3538960 | tf_op jit(solution)/shard_map/all_gather | solution.py:114
  73.6 3.4 convolution_convert_fusion.2
  87.1 4.2 fusion.1
  91.3 5.0 copy.51
  97.0 24.9 %collective-permute-done = bf16[1,768,768]{2,1,0:T(8,128)(2,1)} collective-permute-done((bf16[1,768,768]{2,1,0:T(8,128)(2,1)}, bf16[1,768,768]{2,1,0:T(8,128)(2,1)}, u32[]{:S(2)}, u32[]{:S(2)}) %collective-permute-start) | collective-permute-done | bytes 1179680 | tf_op jit(solution)/shard_map/ppermute | solution.py:27
  126.5 3.0 fusion.66
  132.2 55.1 %all-gather.9.cloned.1.call-done = bf16[768,768]{0,1:T(8,128)(2,1)} async-done(((bf16[768,24]{0,1:T(8,128)(2,1)}), bf16[768,768]{0,1:T(8,128)(2,1)}) %all-gather.9.cloned.1.call-update) | async-done | bytes 1179664 | tf_op jit(solution)/shard_map/all_gather | solution.py:115
  190.2 2.6 gather_fusion
  192.8 2.1 broadcast_select_fusion
  194.9 4.7 all-to-all-start
  202.0 4.1 gather_fusion.4
  206.8 2.6 gather_fusion.3
  210.1 2.3 select_convert_fusion
  212.3 4.1 maximum_bitcast_fusion
  216.4 6.3 gather_fusion.1
  222.8 5.0 all-to-all-start.2
  227.8 17.0 %all-gather.11.cloned.1.call-done = bf16[1,768,3072]{2,1,0:T(8,128)(2,1)} async-done(((bf16[1,768,768]{2,1,0:T(8,128)(2,1)}), bf16[1,768,3072]{2,1,0:T(8,128)(2,1)}) %all-gather.11.cloned.1.call-update) | async-done | bytes 4718608 | tf_op jit(solution)/shard_map/all_gather | solution.py:187
  244.9 4.7 fusion.11
  249.5 2.2 copy-done.37
  251.7 3.7 convolution_convert_fusion.5
  255.4 4.6 all-to-all-start.1
  260.0 6.6 fusion.8
  268.0 5.3 fusion.19
  273.2 3.6 all-to-all-done.1
  276.8 4.2 all-to-all-start.3
  282.6 3.3 gather_fusion.2
  285.9 11.8 %all-to-all-done.3 = bf16[8,48,768]{2,1,0:T(8,128)(2,1)} async-done(((bf16[8,48,768]{2,1,0:T(8,128)(2,1)}), bf16[8,48,768]{2,1,0:T(8,128)(2,1)}, u32[]{:S(2)}, u32[]{:S(2)}) %all-to-all-start.3) | async-done | bytes 589856 | tf_op jit(solution)/shard_map/all_to_all | solution.py:209
  297.8 3.3 gather_fusion.5
  301.1 2.3 reshape.388
  303.3 2.8 reduce_sum.107
  308.5 2.3 reshape.387
  310.8 2.2 multiply_reduce_fusion.1
  313.0 2.0 multiply_add_fusion.1
  325.6 7.7 %fusion.14 = bf16[1,3072,768]{2,1,0:T(8,128)(2,1)} fusion(bf16[384,768]{1,0:T(8,128)(2,1)} %bitcast.30, f32[384,3072]{1,0:T(8,128)} %copy-done.37), kind=kOutput, calls=%fused_computation.28 | convolution fusion | flops 1824915456 | bytes 10027008 | tf_op jit(solution)/shard_map/dot_general | solution.py:59
  335.0 5.6 fusion.13
  341.6 3.1 fusion.48
  344.7 2.5 convolution_convert_fusion.6
  347.2 7.6 %reduce-scatter.16.cloned.1.call-done = bf16[128,1536]{1,0:T(8,128)(2,1)} async-done(((bf16[512,1536]{1,0:T(8,128)(2,1)}), bf16[128,1536]{1,0:T(8,128)(2,1)}) %reduce-scatter.16.cloned.1.call-update) | async-done | bytes 393232
  356.7 5.0 fusion.27
  361.8 3.5 copy.58
  365.3 6.3 fusion.22
  372.5 41.0 %all-reduce.4 = (f32[768]{0:T(1024)S(1)}, f32[32,12]{0,1:T(8,128)}, f32[768]{0:T(1024)S(1)}) all-reduce(f32[768]{0:T(1024)S(1)} %get-tuple-element.11, f32[32,12]{0,1:T(8,128)S(1)} %fusion.22, f32[768]{0:T(1024)S(1)} %copy-done.28), channel_id=3, replica_groups=mesh['dp'=4,'seq'=4,'expert'=2] {'dp','seq','expert'}, use_global_device_ids=true, to_apply=%region_15.16.clone | all-reduce | flops 1920 | bytes 15360
  416.0 2.8 convert_element_type.237
  418.9 57.2 %reduce-scatter.12.cloned.1.call-done = bf16[1,768,768]{2,1,0:T(8,128)(2,1)} async-done(((bf16[1,768,3072]{2,1,0:T(8,128)(2,1)}), bf16[1,768,768]{2,1,0:T(8,128)(2,1)}) %reduce-scatter.12.cloned.1.call-update) | async-done | bytes 1179664 | tf_op jit(solution)/shard_map/reduce_scatter | solution.py:194
  476.0 2.8 convert_element_type.234
  478.9 102.6 %reduce-scatter.10.cloned.1.call-done = f32[768,24]{0,1:T(8,128)} async-done(((f32[768,768]{0,1:T(8,128)}), f32[768,24]{0,1:T(8,128)}) %reduce-scatter.10.cloned.1.call-update) | async-done | bytes 73744 | tf_op jit(solution)/shard_map/reduce_scatter | solution.py:283
  581.5 124.9 %reduce-scatter.8.cloned.1.call-done = f32[768,72]{0,1:T(8,128)} async-done(((f32[768,2304]{0,1:T(8,128)}), f32[768,72]{0,1:T(8,128)}) %reduce-scatter.8.cloned.1.call-update) | async-done | bytes 221200 | tf_op jit(solution)/shard_map/reduce_scatter | solution.py:282
  (173 shorter events, 51.9 us)
Async XLA Ops:
  7.2 79.9 %copy-start = (f32[32,12]{0,1:T(8,128)S(1)}, f32[32,12]{0,1:T(8,128)}, u32[]{:S(2)}) copy-start(f32[32,12]{0,1:T(8,128)} %param.19) | copy-start | bytes 4612
  7.2 66.4 %all-gather.5.cloned.1.call-start = ((), (), s32[]{:S(2)}) async-start(), calls=%async_computation.9 | async-start | bytes 3649536 | tf_op jit(solution)/shard_map/all_gather | solution.py:114
  7.9 114.7 %all-gather.7.cloned.1.call-start = ((), (), s32[]{:S(2)}) async-start(), calls=%async_computation.10 | async-start | bytes 1966080 | tf_op jit(solution)/shard_map/all_gather | solution.py:126
  52.5 26.7 %copy-start.24 = (f32[768]{0:T(1024)}, f32[768]{0:T(1024)S(1)}, u32[]{:S(2)}) copy-start(f32[768]{0:T(1024)S(1)} %convert_element_type.196) | copy-start | bytes 9220
  53.6 25.5 %copy-start.29 = (f32[128]{0:T(128)}, f32[128]{0:T(128)S(1)}, u32[]{:S(2)}) copy-start(f32[128]{0:T(128)S(1)} %add_rsqrt_fusion.1) | copy-start | bytes 1540
  53.6 28.5 %copy-start.34 = (s32[1,128,2]{1,2,0:T(2,128)S(1)}, s32[1,128,2]{1,2,0:T(2,128)}, u32[]{:S(2)}) copy-start(s32[1,128,2]{1,2,0:T(2,128)} %param.14) | copy-start | bytes 3076
  77.8 109.5 %all-gather.9.cloned.1.call-start = ((), (), s32[]{:S(2)}) async-start(), calls=%async_computation.11 | async-start | bytes 1216512 | tf_op jit(solution)/shard_map/all_gather | solution.py:115
  78.6 166.3 %all-gather.11.cloned.1.call-start = ((), (), s32[]{:S(2)}) async-start(), calls=%async_computation.12 | async-start | bytes 5898240 | tf_op jit(solution)/shard_map/all_gather | solution.py:187
  79.2 42.7 %collective-permute-start = (bf16[1,768,768]{2,1,0:T(8,128)(2,1)}, bf16[1,768,768]{2,1,0:T(8,128)(2,1)}, u32[]{:S(2)}, u32[]{:S(2)}) collective-permute-start(bf16[1,768,768]{2,1,0:T(8,128)(2,1)} %param.22), channel_id=1, source_target_pairs={{0,2},{2,4},{4,6},{6,0},{1,3},{3,5},{5,7},{7,1},{8,10},{10,12},{12... | collective-permute-start | bytes 3538952 | tf_op jit(solution)/shard_map/ppermute | solution.py:27
  80.6 131.7 %collective-permute-start.2 = (bf16[1,768,768]{2,1,0:T(8,128)(2,1)}, bf16[1,768,768]{2,1,0:T(8,128)(2,1)}, u32[]{:S(2)}, u32[]{:S(2)}) collective-permute-start(bf16[1,768,768]{2,1,0:T(8,128)(2,1)} %param.22), channel_id=1, source_target_pairs={{2,0},{4,2},{6,4},{0,6},{3,1},{5,3},{7,5},{1,7},{10,8},{12,10},{14... | collective-permute-start | bytes 3538952 | tf_op jit(solution)/shard_map/ppermute | solution.py:29
  84.4 2.1 copy-start.35
  87.1 9.1 %copy-start.17 = (s32[128,512]{0,1:T(8,128)}, s32[128,512]{0,1:T(8,128)S(1)}, u32[]{:S(2)}) copy-start(s32[128,512]{0,1:T(8,128)S(1)} %copy.50) | copy-start | bytes 786436
  91.3 5.0 copy-start.36
  97.0 29.5 %copy-start.21 = (pred[128,512]{1,0:T(8,128)(4,1)}, pred[128,512]{1,0:T(8,128)(4,1)S(1)}, u32[]{:S(2)}) copy-start(pred[128,512]{1,0:T(8,128)(4,1)S(1)} %fusion.45) | copy-start | bytes 196612
  121.9 90.4 %collective-permute-start.1 = (bf16[1,768,768]{2,1,0:T(8,128)(2,1)}, bf16[1,768,768]{2,1,0:T(8,128)(2,1)}, u32[]{:S(2)}, u32[]{:S(2)}) collective-permute-start(bf16[1,768,768]{2,1,0:T(8,128)(2,1)} %collective-permute-done), channel_id=1, source_target_pairs={{0,2},{2,4},{4,6},{6,0},{1,3},{3,5},{5,7},{7,1},{8,10},{10,12},{12... | collective-permute-start | bytes 3538952 | tf_op jit(solution)/shard_map/ppermute | solution.py:27
  122.6 3.9 copy-start.19
  129.5 57.8 %copy-start.5 = (f32[1,128,768]{2,1,0:T(8,128)S(1)}, f32[1,128,768]{2,1,0:T(8,128)}, u32[]{:S(2)}) copy-start(f32[1,128,768]{2,1,0:T(8,128)} %param.12) | copy-start | bytes 1179652
  130.7 59.4 %copy-start.26 = (f32[768]{0:T(1024)S(1)}, f32[768]{0:T(1024)}, u32[]{:S(2)}) copy-start(f32[768]{0:T(1024)} %convert_element_type.218) | copy-start | bytes 9220
  130.7 59.5 %copy-start.27 = (s32[1024]{0:T(1024)S(1)}, s32[1024]{0:T(1024)}, u32[]{:S(2)}) copy-start(s32[1024]{0:T(1024)} %get-tuple-element.32) | copy-start | bytes 12292
  192.8 14.0 %copy-start.2 = (f32[1,128,768]{2,1,0:T(8,128)S(1)}, f32[1,128,768]{2,1,0:T(8,128)}, u32[]{:S(2)}) copy-start(f32[1,128,768]{2,1,0:T(8,128)} %param.23) | copy-start | bytes 1179652
  194.9 27.8 %all-to-all-start = ((bf16[8,48,768]{2,1,0:T(8,128)(2,1)}), bf16[8,48,768]{2,1,0:T(8,128)(2,1)}, u32[]{:S(2)}, u32[]{:S(2)}) async-start(bf16[8,48,768]{2,1,0:T(8,128)(2,1)} %broadcast_select_fusion), calls=%async_computation | async-start | bytes 1179648 | tf_op jit(solution)/shard_map/all_to_all | solution.py:177
  222.8 32.6 %all-to-all-start.2 = ((bf16[8,48,768]{2,1,0:T(8,128)(2,1)}), bf16[8,48,768]{2,1,0:T(8,128)(2,1)}, u32[]{:S(2)}, u32[]{:S(2)}) async-start(bf16[8,48,768]{2,1,0:T(8,128)(2,1)} %select_convert_fusion), calls=%async_computation.2 | async-start | bytes 1179648 | tf_op jit(solution)/shard_map/all_to_all | solution.py:180
  244.9 6.9 copy-start.12
  249.5 2.2 copy-start.37
  255.4 21.4 %all-to-all-start.1 = ((bf16[8,48,768]{2,1,0:T(8,128)(2,1)}), bf16[8,48,768]{2,1,0:T(8,128)(2,1)}, u32[]{:S(2)}, u32[]{:S(2)}) async-start(bf16[8,48,768]{2,1,0:T(8,128)(2,1)} %bitcast.136), calls=%async_computation.1 | async-start | bytes 1179648 | tf_op jit(solution)/shard_map/all_to_all | solution.py:202
  268.0 13.3 %copy-start.33 = (f32[1,128,2]{1,2,0:T(2,128)S(1)}, f32[1,128,2]{1,2,0:T(2,128)}, u32[]{:S(2)}) copy-start(f32[1,128,2]{1,2,0:T(2,128)} %param.15) | copy-start | bytes 3076
  276.8 20.9 %all-to-all-start.3 = ((bf16[8,48,768]{2,1,0:T(8,128)(2,1)}), bf16[8,48,768]{2,1,0:T(8,128)(2,1)}, u32[]{:S(2)}, u32[]{:S(2)}) async-start(bf16[8,48,768]{2,1,0:T(8,128)(2,1)} %bitcast.135), calls=%async_computation.3 | async-start | bytes 1179648 | tf_op jit(solution)/shard_map/all_to_all | solution.py:209
  281.0 73.8 %reduce-scatter.16.cloned.1.call-start = ((), (), s32[]{:S(2)}) async-start(), calls=%async_computation.17 | async-start | bytes 1966080
  301.1 11.9 %copy-start.32 = (f32[128]{0:T(128)S(1)}, f32[128]{0:T(128)}, u32[]{:S(2)}) copy-start(f32[128]{0:T(128)} %copy-done.31) | copy-start | bytes 1540
  310.8 5.1 copy-start.13
  315.8 3.8 copy-start.23
  317.9 1.7 copy-start.16
  320.8 2.7 copy-start.20
  321.8 1.7 copy-start.3
  325.6 90.4 %reduce-scatter.14.cloned.1.call-start = ((), (), s32[]{:S(2)}) async-start(), calls=%async_computation.16 | async-start | bytes 5898240 | tf_op jit(solution)/shard_map/reduce_scatter | solution.py:197
  333.3 1.7 copy-start.39
  333.4 142.7 %reduce-scatter.12.cloned.1.call-start = ((), (), s32[]{:S(2)}) async-start(), calls=%async_computation.15 | async-start | bytes 5898240 | tf_op jit(solution)/shard_map/reduce_scatter | solution.py:194
  340.6 4.1 copy-start.4
  340.6 240.9 %reduce-scatter.10.cloned.1.call-start = ((), (), s32[]{:S(2)}) async-start(), calls=%async_computation.14 | async-start | bytes 2433024 | tf_op jit(solution)/shard_map/reduce_scatter | solution.py:283
  344.6 12.1 %copy-start.6 = (f32[1,128,768]{2,1,0:T(8,128)S(1)}, f32[1,128,768]{2,1,0:T(8,128)}, u32[]{:S(2)}) copy-start(f32[1,128,768]{2,1,0:T(8,128)} %param.12) | copy-start | bytes 1179652
  344.6 12.1 %copy-start.25 = (f32[768]{0:T(1024)S(1)}, f32[768]{0:T(1024)}, u32[]{:S(2)}) copy-start(f32[768]{0:T(1024)} %copy-done.24) | copy-start | bytes 9220
  344.6 12.1 %copy-start.30 = (f32[128]{0:T(128)S(1)}, f32[128]{0:T(128)}, u32[]{:S(2)}) copy-start(f32[128]{0:T(128)} %copy-done.29) | copy-start | bytes 1540
  344.7 361.7 %reduce-scatter.8.cloned.1.call-start = ((), (), s32[]{:S(2)}) async-start(), calls=%async_computation.13 | async-start | bytes 7299072 | tf_op jit(solution)/shard_map/reduce_scatter | solution.py:282
  365.3 6.3 copy-start.7
  365.3 6.3 copy-start.14
  365.3 6.3 copy-start.18
  371.7 43.0 %copy-start.11 = (f32[128,768]{1,0:T(8,128)S(1)}, f32[128,768]{1,0:T(8,128)}, u32[]{:S(2)}) copy-start(f32[128,768]{1,0:T(8,128)} %copy-done.9) | copy-start | bytes 1179652
  414.7 291.7 %copy-start.1 = (f32[32,12]{0,1:T(8,128)S(1)}, f32[32,12]{0,1:T(8,128)}, u32[]{:S(2)}) copy-start(f32[32,12]{0,1:T(8,128)} %param.19) | copy-start | bytes 4612
  (8 other events, 7.8 us)
Sparse Core Ops, SparseCore 0:
  10.9 62.6 all-gather.4
  78.0 42.8 all-gather.6
  123.7 63.5 all-gather.8
  189.0 55.8 all-gather.10
  325.7 29.0 reduce-scatter.15
  357.7 58.3 reduce-scatter.13
  419.0 56.9 reduce-scatter.11
  481.9 99.5 reduce-scatter.9
  587.8 118.5 reduce-scatter.7
